TPU v7x, 128 devices: a whole 4x4x4 slice. The times are simulated.
128 devices in a mesh: dp: 16 (over y_hi, z, core), tensor: 8 (over x, y_lo).
Axes of the slice: x: 4, y: 4 (y_hi: 2, y_lo: 2; y = y_hi * 2 + y_lo), z: 4, core: 2. Of those that a mesh axis runs over, the one named last changes fastest.
Arguments:
- activations: bfloat16 [16384, 8192], P('dp'), may hold values from -6 to 6
- out_grad: bfloat16 [16384, 28672], P('dp', 'tensor'), may hold values from -0.046875 to 0.046875
- projector: bfloat16 [8192, 512], P(('dp', 'tensor')), may hold values from -0.0625 to 0.0625
- first_moment: float32 [512, 28672], P('dp', 'tensor'), may hold values from -3 to 3
- second_moment: float32 [512, 28672], P('dp', 'tensor'), may hold values from 0.1 to 4
Outputs:
- update: float32 [8192, 28672], P('dp', 'tensor')
- new_first: float32 [512, 28672], P('dp', 'tensor')
- new_second: float32 [512, 28672], P('dp', 'tensor')
All inputs are finite; a program needn't handle non-finite values.
Results may differ from a plain program's by a relative error of at most 0.0031.
Values may be sent and summed in bfloat16 or wider, within the bound.
A program may use at most 128 MiB of HBM per device.

v0:
```python
import jax
import jax.numpy as jnp
from jax import lax
from jax.sharding import PartitionSpec as P

beta_one = 0.9
beta_two = 0.999
bias_one = 1.0 - 0.9**10
bias_two = 1.0 - 0.999**10
adam_eps = 1e-08


def in_order(tiles, dim):
    dims = list(tiles.shape[1:])
    dims[dim] *= tiles.shape[0]
    return jnp.moveaxis(tiles, 0, dim).reshape(dims)


def sent_to_all(shard, axis):
    copies = jnp.broadcast_to(shard, (lax.axis_size(axis), *shard.shape))
    return lax.all_to_all(copies, axis, split_axis=0, concat_axis=0, tiled=True)


def collect(shard, axis, dim):
    return in_order(sent_to_all(shard, axis), dim)


def per_device(activations, out_grad, projector, first_moment, second_moment):
    token_rows = activations.shape[0]
    lane_blocks = collect(projector, "dp", 0)
    data_lanes = lax.axis_size("dp")
    tensor_lanes = lax.axis_size("tensor")
    block_rows = projector.shape[0]
    split_cols = activations.reshape(token_rows, data_lanes, tensor_lanes, block_rows)
    chosen = lax.dynamic_index_in_dim(split_cols, lax.axis_index("tensor"), 2, keepdims=False)
    chosen = chosen.reshape(token_rows, data_lanes * block_rows)
    partial_sum = jnp.dot(chosen, lane_blocks, preferred_element_type=jnp.float32)
    projected = lax.psum(partial_sum, "tensor")
    projected = projected.astype(jnp.bfloat16)
    coefficients = lax.psum_scatter(
        lax.dot_general(
            projected, out_grad, (((0,), (0,)), ((), ())), preferred_element_type=jnp.float32
        ),
        "dp",
        scatter_dimension=0,
        tiled=True,
    )
    new_first = beta_one * first_moment + (1.0 - beta_one) * coefficients
    new_second = beta_two * second_moment + (1.0 - beta_two) * coefficients * coefficients
    normalized = (new_first / bias_one / (jnp.sqrt(new_second / bias_two) + adam_eps)).astype(
        jnp.bfloat16
    )
    basis_rows = collect(projector, "tensor", 0)
    update = jnp.dot(
        basis_rows,
        lax.all_gather(normalized, "dp", axis=0, tiled=True),
        preferred_element_type=jnp.float32,
    )
    return (update, new_first, new_second)


def solution(mesh):
    in_specs = (
        P("dp", None),
        P("dp", "tensor"),
        P(("dp", "tensor"), None),
        P("dp", "tensor"),
        P("dp", "tensor"),
    )
    out_specs = (P("dp", "tensor"), P("dp", "tensor"), P("dp", "tensor"))
    return jax.shard_map(
        per_device, mesh=mesh, in_specs=in_specs, out_specs=out_specs, check_vma=False
    )
```

profile of v0, /device:TPU:1, one launch (start us, length us, event | category | flops | bytes accessed | tf_op | source)
XLA Modules:
  0.0 319.9 jit_solution(16738832030383836894)
XLA Ops:
  7.2 1.9 broadcast_in_dim.6
  9.1 9.4 %all-to-all-start = ((bf16[16,64,512]{2,1,0:T(8,128)(2,1)}), bf16[16,64,512]{2,1,0:T(8,128)(2,1)S(1)}, u32[]{:S(2)}, u32[]{:S(2)}) async-start(bf16[16,64,512]{2,1,0:T(8,128)(2,1)} %broadcast_in_dim.6), calls=%async_computation | async-start | bytes 2097152 | tf_op jit(solution)/shard_map/all_to_all | solution.py:21
  18.5 0.0 reduce-scatter.2.cloned.1.call-start
  18.6 22.4 %copy.9 = bf16[1024,8192]{0,1:T(8,128)(2,1)} copy(bf16[1024,8192]{1,0:T(8,128)(2,1)} %param.5) | data formatting | bytes 33554432 | tf_op args[0]
  41.0 3.1 constant_dynamic-slice_fusion
  44.2 0.0 all-to-all-done
  44.2 2.9 fusion.4
  47.0 84.2 %all-reduce.1 = bf16[1024,512]{1,0:T(8,128)(2,1)S(1)} all-reduce(f32[1024,512]{1,0:T(8,128)S(1)} %fusion.4), channel_id=1, replica_groups=mesh['dp'=16,'tensor'=8] {'tensor'}, use_global_device_ids=true, to_apply=%region_0.1 | all-reduce | flops 524288 | bytes 3145728 | tf_op jit(solution)/shard_map/psum | solution.py:38
  131.3 9.2 %fusion.5 = f32[512,3584]{1,0:T(8,128)} fusion(bf16[1024,512]{1,0:T(8,128)(2,1)S(1)} %all-reduce.1, bf16[1024,3584]{1,0:T(8,128)(2,1)} %param.6), kind=kOutput, calls=%fused_computation.9 | convolution fusion | flops 3758096384 | bytes 15728640 | tf_op jit(solution)/shard_map/dot_general | solution.py:41
  140.4 0.0 copy-start
  140.4 0.0 copy-start.1
  140.4 0.0 copy-start.2
  140.4 0.0 reduce-scatter.2.cloned.1.call-update
  140.5 0.0 all-gather.2.cloned.1.call-start
  140.5 100.7 %reduce-scatter.2.cloned.1.call-done = f32[32,3584]{1,0:T(8,128)} async-done(((f32[512,3584]{1,0:T(8,128)}), f32[32,3584]{1,0:T(8,128)}) %reduce-scatter.2.cloned.1.call-update) | async-done | bytes 458768 | tf_op jit(solution)/shard_map/reduce_scatter | solution.py:40
  241.2 0.0 copy-done
  241.2 0.0 copy-done.1
  241.2 2.2 divide_convert_fusion
  243.4 0.0 all-gather.2.cloned.1.call-update
  243.4 0.0 copy-done.2
  243.5 11.2 %all_to_all.10 = bf16[8,64,512]{2,1,0:T(8,128)(2,1)S(1)} all-to-all(bf16[8,64,512]{2,1,0:T(8,128)(2,1)S(1)} %broadcast_in_dim.7), channel_id=1, replica_groups=mesh['dp'=16,'tensor'=8] {'tensor'}, dimensions={0} | all-to-all | bytes 1048576 | tf_op jit(solution)/shard_map/all_to_all | solution.py:21
  254.7 42.9 %all-gather.2.cloned.1.call-done = bf16[512,3584]{1,0:T(8,128)(2,1)} async-done(((bf16[32,3584]{1,0:T(8,128)(2,1)}), bf16[512,3584]{1,0:T(8,128)(2,1)}) %all-gather.2.cloned.1.call-update) | async-done | bytes 3670032 | tf_op jit(solution)/shard_map/all_gather | solution.py:56
  297.6 7.1 %convolution_bitcast_fusion = f32[512,3584]{0,1:T(8,128)} fusion(bf16[512,3584]{1,0:T(8,128)(2,1)} %all-gather.2.cloned.1.call-done, bf16[512,512]{1,0:T(8,128)(2,1)S(1)} %bitcast.13), kind=kOutput, calls=%fused_computation | convolution fusion | flops 1879048192 | bytes 11534336 | tf_op jit(solution)/shard_map/dot_general | solution.py:54
  304.7 8.4 %copy.10 = f32[512,3584]{1,0:T(8,128)} copy(f32[512,3584]{0,1:T(8,128)} %convolution_bitcast_fusion) | data formatting | bytes 14680064
  (1 shorter events, 0.0 us)
Async XLA Ops:
  9.1 35.1 %all-to-all-start = ((bf16[16,64,512]{2,1,0:T(8,128)(2,1)}), bf16[16,64,512]{2,1,0:T(8,128)(2,1)S(1)}, u32[]{:S(2)}, u32[]{:S(2)}) async-start(bf16[16,64,512]{2,1,0:T(8,128)(2,1)} %broadcast_in_dim.6), calls=%async_computation | async-start | bytes 2097152 | tf_op jit(solution)/shard_map/all_to_all | solution.py:21
  18.5 222.7 %reduce-scatter.2.cloned.1.call-start = ((), (), s32[]{:S(2)}) async-start(), calls=%async_computation.3 | async-start | bytes 7798784 | tf_op jit(solution)/shard_map/reduce_scatter | solution.py:40
  140.4 100.8 %copy-start = (f32[32,3584]{1,0:T(8,128)S(1)}, f32[32,3584]{1,0:T(8,128)}, u32[]{:S(2)}) copy-start(f32[32,3584]{1,0:T(8,128)} %param.8) | copy-start | bytes 1376260
  140.4 100.8 %copy-start.1 = (f32[32,3584]{1,0:T(8,128)S(1)}, f32[32,3584]{1,0:T(8,128)}, u32[]{:S(2)}) copy-start(f32[32,3584]{1,0:T(8,128)} %param.9) | copy-start | bytes 1376260
  140.4 103.0 %copy-start.2 = (bf16[64,512]{1,0:T(8,128)(2,1)S(1)}, bf16[64,512]{1,0:T(8,128)(2,1)}, u32[]{:S(2)}) copy-start(bf16[64,512]{1,0:T(8,128)(2,1)} %param.7) | copy-start | bytes 196612
  140.5 157.1 %all-gather.2.cloned.1.call-start = ((), (), s32[]{:S(2)}) async-start(), calls=%async_computation.4 | async-start | bytes 3899392 | tf_op jit(solution)/shard_map/all_gather | solution.py:56
Sparse Core Ops, SparseCore 0:
  140.6 100.6 reduce-scatter.1
  244.3 53.2 all-gather.1
where the time goes:
time: 321 us; the launch traced here: 320 us
  waiting for transfers between devices  144 us (45%)
  blocking collectives  95.4 us (30%)
  local copies, waits for them, and re-layouts  35.9 us (11%)
  matrix products  19.1 us (6%)
  between operations  14.1 us (4%)
  starting transfers between devices  9.53 us (3%)
    reduce_scatter x1, waiting for transfers between devices, per_device(): lax.psum_scatter(lax.dot_general(projected, out_grad, (((0,), (0,)), ((),...  101 us
    psum x1, blocking collectives, per_device(): projected = lax.psum(partial_sum, 'tensor')  84.2 us
    all_gather x1, waiting for transfers between devices, per_device(): lax.all_gather(normalized, 'dp', axis=0, tiled=True)  42.9 us
    unnamed x8, local copies, waits for them, and re-layouts  30.8 us
    all_to_all x1, blocking collectives, sent_to_all(): return lax.all_to_all(copies, axis, split_axis=0, concat_axis=0, tiled=True)  11.2 us
    all_to_all x1, starting transfers between devices, sent_to_all(): return lax.all_to_all(copies, axis, split_axis=0, concat_axis=0, tiled=True)  9.45 us
    dot_general x1, matrix products, per_device(): lax.dot_general(projected, out_grad, (((0,), (0,)), ((), ())), preferred_...  9.15 us
    dot_general x1, matrix products, per_device(): jnp.dot(basis_rows, lax.all_gather(normalized, 'dp', axis=0, tiled=True),...  7.12 us
  transfers between devices with their start and end apart: 3, of which 2 were waited for; matrix products, arithmetic and copies ran while one was open for 8% of the time, Pallas kernels for 0%

commit v1 on v0

v1 whole, which is shorter than its diff:
```python
import jax
import jax.numpy as jnp
from jax import lax
from jax.experimental import pallas as pl
from jax.experimental.pallas import tpu as pltpu
from jax.sharding import PartitionSpec as P

beta_one = 0.9
beta_two = 0.999
bias_one = 1.0 - 0.9**10
bias_two = 1.0 - 0.999**10
adam_eps = 1e-08

MESH = pl.DeviceIdType.MESH
CHUNKS = 7
STEP = 256
NT = (((1,), (1,)), ((), ()))


def fused(act_hbm, grad_hbm, proj_ref, first_ref, second_ref,
          norm_ref, basis_ref, nfirst_ref, nsecond_ref,
          act, grad, slices, acc, pj, th_out, th_in, mine, rs_out, rs_in,
          act_sem, grad_sem, local_sem,
          a_s, a_r, b_s, b_r, f_s, f_r, c_s, c_r, t_s, t_r, r_s, r_r, g_s, g_r, h_s, h_r):
    dp = lax.axis_index("dp")
    tn = lax.axis_index("tensor")
    chip, core = dp // 2, dp % 2
    rows = proj_ref.shape[0]
    width = act.shape[2]
    cols = grad.shape[2]
    half = pj.shape[1]
    own = half // 8

    def chip_to(i):
        return ((chip // 4 + i // 4) % 2) * 4 + (chip % 4 + i % 4) % 4

    def chip_from(i):
        return ((chip // 4 + i // 4) % 2) * 4 + (chip % 4 + 4 - i % 4) % 4

    def tensor_to(i):
        return ((tn // 2 + i // 2) % 4) * 2 + (tn % 2 + i % 2) % 2

    partner = {"dp": chip * 2 + (1 - core)}

    def act_copy(k):
        return pltpu.make_async_copy(
            act_hbm.at[:, pl.ds(pl.multiple_of(k * width, 128), width)], act.at[k], act_sem.at[k])

    def grad_copy(j):
        return pltpu.make_async_copy(
            grad_hbm.at[:, pl.ds(pl.multiple_of(j * cols, 128), cols)], grad.at[j], grad_sem.at[j])

    for k in range(16):
        act_copy(k).start()
    for j in range(CHUNKS):
        grad_copy(j).start()
    my_rows = pl.ds(pl.multiple_of(tn * rows, 16), rows)
    local = pltpu.make_async_copy(proj_ref, basis_ref.at[my_rows], local_sem)
    local.start()

    barrier = pltpu.get_barrier_semaphore()
    for i in range(1, 8):
        pl.semaphore_signal(barrier, inc=1, device_id={"tensor": tensor_to(i)}, device_id_type=MESH)
        pl.semaphore_signal(barrier, inc=1, device_id={"dp": chip_to(i) * 2 + core}, device_id_type=MESH)
    pl.semaphore_signal(barrier, inc=1, device_id=partner, device_id_type=MESH)
    pl.semaphore_wait(barrier, 15)

    def a_copy(i):
        return pltpu.make_async_remote_copy(
            proj_ref, basis_ref.at[my_rows], a_s.at[i], a_r.at[i],
            device_id={"tensor": tensor_to(i)}, device_id_type=MESH)

    for i in range(1, 8):
        a_copy(i).start()
    local.wait()
    for i in range(1, 8):
        a_copy(i).wait_recv()

    ranks = slices.shape[1]
    pick = (lax.broadcasted_iota(jnp.int32, (ranks, basis_ref.shape[1]), 1)
            == lax.broadcasted_iota(jnp.int32, (ranks, basis_ref.shape[1]), 0) + tn * ranks)
    pick = jnp.where(pick, 1.0, 0.0).astype(jnp.bfloat16)
    slices[dp] = lax.dot_general(
        pick, basis_ref[...], NT, preferred_element_type=jnp.float32).astype(jnp.bfloat16)

    def b_copy(i):
        return pltpu.make_async_remote_copy(
            slices.at[dp], slices.at[dp], b_s.at[i], b_r.at[i],
            device_id={"dp": chip_to(i) * 2 + core}, device_id_type=MESH)

    b_pair = pltpu.make_async_remote_copy(
        slices.at[dp], slices.at[dp], b_s.at[0], b_r.at[0], device_id=partner, device_id_type=MESH)

    def f_copy(i):
        src = chip_from(i) * 2 + core
        return pltpu.make_async_remote_copy(
            slices.at[src], slices.at[src], f_s.at[i], f_r.at[i], device_id=partner, device_id_type=MESH)

    for i in range(1, 8):
        b_copy(i).start()
    b_pair.start()

    def wait_act(k, _):
        act_copy(k).wait()
        return 0

    lax.fori_loop(0, 16, wait_act, 0)

    def project(k):
        acc[...] += lax.dot_general(act[k], slices[k], NT, preferred_element_type=jnp.float32)

    acc[...] = jnp.zeros_like(acc)

    def near(i, _):
        @pl.when(i == 1)
        def _():
            b_pair.wait_recv()
        project(chip * 2 + (core + i) % 2)
        return 0

    lax.fori_loop(0, 2, near, 0)

    def arrived(i, _):
        b_copy(i).wait_recv()
        f_copy(i).start()
        project(chip_from(i) * 2 + core)
        return 0

    lax.fori_loop(1, 8, arrived, 0)

    def forwarded(i, _):
        f_copy(i).wait_recv()
        project(chip_from(i) * 2 + (1 - core))
        return 0

    lax.fori_loop(1, 8, forwarded, 0)

    mine_rows = pl.ds(pl.multiple_of(tn * own, 16), own)
    done = acc[...].T.astype(jnp.bfloat16)
    pj[0, mine_rows] = done[:own]
    pj[1, mine_rows] = done[own:]

    def c_copy(h, i):
        side = (core + 1 + h) % 2
        return pltpu.make_async_remote_copy(
            pj.at[side, mine_rows], pj.at[side, mine_rows], c_s.at[h, i], c_r.at[h, i],
            device_id={"tensor": tensor_to(i)}, device_id_type=MESH)

    def c_wait(h, i):
        src = ((tn // 2 + 4 - i // 2) % 4) * 2 + (tn % 2 + i % 2) % 2
        there = pl.ds(pl.multiple_of(src * own, 16), own)
        side = (core + 1) % 2 if h == 0 else core
        pltpu.make_async_remote_copy(
            pj.at[side, there], pj.at[side, there], c_s.at[h, i], c_r.at[h, i],
            device_id={"tensor": tensor_to(i)}, device_id_type=MESH).wait_recv()

    for h in range(2):
        for i in range(1, 8):
            c_copy(h, i).start()
    for j in range(CHUNKS):
        grad_copy(j).wait()

    def t_copy(j):
        return pltpu.make_async_remote_copy(
            th_out.at[j], th_in.at[j], t_s.at[j], t_r.at[j], device_id=partner, device_id_type=MESH)

    for i in range(1, 8):
        c_wait(0, i)

    def theirs(j, _):
        for s in range(0, cols, STEP):
            th_out[j, :, s:s + STEP] = jnp.dot(
                pj[1 - core], grad[j, :, s:s + STEP], preferred_element_type=jnp.float32)
        t_copy(j).start()
        return 0

    lax.fori_loop(0, CHUNKS, theirs, 0)

    for i in range(1, 8):
        c_wait(1, i)

    def r_copy(j, i):
        return pltpu.make_async_remote_copy(
            rs_out.at[j, chip_to(i)], rs_in.at[j, i], r_s.at[j, i], r_r.at[j, i],
            device_id={"dp": chip_to(i) * 2 + core}, device_id_type=MESH)

    def ours(j, _):
        t_copy(j).wait_recv()
        for s in range(0, cols, STEP):
            total = jnp.dot(pj[core], grad[j, :, s:s + STEP], preferred_element_type=jnp.float32)
            total += th_in[j, :, s:s + STEP]
            total = total.reshape(8, own, STEP)
            mine[j, :, :, s:s + STEP] = total
            rs_out[j, :, :, s:s + STEP] = total.astype(jnp.bfloat16)
        for i in range(1, 8):
            r_copy(j, i).start()
        return 0

    lax.fori_loop(0, CHUNKS, ours, 0)

    out_rows = pl.ds(pl.multiple_of(dp * own, 16), own)

    def g_copy(j, i):
        to = partner if i is None else {"dp": chip_to(i) * 2 + core}
        k = 0 if i is None else i
        return pltpu.make_async_remote_copy(
            norm_ref.at[j, out_rows], norm_ref.at[j, out_rows], g_s.at[j, k], g_r.at[j, k],
            device_id=to, device_id_type=MESH)

    def h_copy(j, i):
        there = pl.ds(pl.multiple_of((chip_from(i) * 2 + core) * own, 16), own)
        return pltpu.make_async_remote_copy(
            norm_ref.at[j, there], norm_ref.at[j, there], h_s.at[j, i], h_r.at[j, i],
            device_id=partner, device_id_type=MESH)

    def adam(j, _):
        for i in range(1, 8):
            r_copy(j, i).wait_recv()
        total = mine[j, chip]
        for i in range(1, 8):
            total += rs_in[j, i].astype(jnp.float32)
        at = pl.ds(pl.multiple_of(j * cols, 128), cols)
        new_first = beta_one * first_ref[:, at] + (1.0 - beta_one) * total
        new_second = beta_two * second_ref[:, at] + (1.0 - beta_two) * total * total
        nfirst_ref[:, at] = new_first
        nsecond_ref[:, at] = new_second
        norm_ref[j, out_rows] = (
            new_first / bias_one / (jnp.sqrt(new_second / bias_two) + adam_eps)).astype(jnp.bfloat16)
        for i in range(1, 8):
            g_copy(j, i).start()
        g_copy(j, None).start()
        return 0

    lax.fori_loop(0, CHUNKS, adam, 0)

    def pass_on(j, _):
        for i in range(1, 8):
            g_copy(j, i).wait_recv()
            h_copy(j, i).start()
        return 0

    lax.fori_loop(0, CHUNKS, pass_on, 0)

    def finish(j, _):
        g_copy(j, None).wait()
        t_copy(j).wait_send()
        for i in range(1, 8):
            h_copy(j, i).wait()
            g_copy(j, i).wait_send()
            r_copy(j, i).wait_send()
        return 0

    lax.fori_loop(0, CHUNKS, finish, 0)
    b_pair.wait_send()
    for i in range(1, 8):
        a_copy(i).wait_send()
        b_copy(i).wait_send()
        f_copy(i).wait_send()
        for h in range(2):
            c_copy(h, i).wait_send()


def decode(basis_ref, norm_ref, nf_ref, ns_ref, update_ref, nf_out, ns_out):
    update_ref[...] = jnp.dot(basis_ref[...], norm_ref[0], preferred_element_type=jnp.float32)
    nf_out[...] = nf_ref[...]
    ns_out[...] = ns_ref[...]


def per_device(activations, out_grad, projector, first_moment, second_moment):
    tokens, width = activations.shape
    ff = out_grad.shape[1]
    rows, rank = projector.shape
    own = first_moment.shape[0]
    cols = ff // CHUNKS
    half = rank // 2
    bf, f32 = jnp.bfloat16, jnp.float32
    vmem = pl.BlockSpec(memory_space=pltpu.VMEM)
    any_ = pl.BlockSpec(memory_space=pl.ANY)
    dma = pltpu.SemaphoreType.DMA
    norm, basis, nf, ns = pl.pallas_call(
        fused,
        out_shape=(
            jax.ShapeDtypeStruct((CHUNKS, rank, cols), bf),
            jax.ShapeDtypeStruct((rows * 8, rank), bf),
            jax.ShapeDtypeStruct(first_moment.shape, f32),
            jax.ShapeDtypeStruct(second_moment.shape, f32),
        ),
        in_specs=[any_, any_, vmem, vmem, vmem],
        out_specs=(vmem, vmem, vmem, vmem),
        scratch_shapes=[
            pltpu.VMEM((16, tokens, width // 16), bf),
            pltpu.VMEM((CHUNKS, tokens, cols), bf),
            pltpu.VMEM((16, rank // 8, width // 16), bf),
            pltpu.VMEM((tokens, rank // 8), f32),
            pltpu.VMEM((2, half, tokens), bf),
            pltpu.VMEM((CHUNKS, half, cols), f32),
            pltpu.VMEM((CHUNKS, half, cols), f32),
            pltpu.VMEM((CHUNKS, 8, own, cols), f32),
            pltpu.VMEM((CHUNKS, 8, own, cols), bf),
            pltpu.VMEM((CHUNKS, 8, own, cols), bf),
            dma((16,)), dma((CHUNKS,)), dma,
            dma((8,)), dma((8,)), dma((8,)), dma((8,)), dma((8,)), dma((8,)),
            dma((2, 8)), dma((2, 8)), dma((CHUNKS,)), dma((CHUNKS,)),
            dma((CHUNKS, 8)), dma((CHUNKS, 8)), dma((CHUNKS, 8)), dma((CHUNKS, 8)),
            dma((CHUNKS, 8)), dma((CHUNKS, 8)),
        ],
        compiler_params=pltpu.CompilerParams(
            collective_id=0, has_side_effects=True, vmem_limit_bytes=60 * 2**20),
        name="fused",
    )(activations, out_grad, projector, first_moment, second_moment)
    return pl.pallas_call(
        decode,
        grid=(CHUNKS,),
        out_shape=(
            jax.ShapeDtypeStruct((rows * 8, ff), f32),
            jax.ShapeDtypeStruct(first_moment.shape, f32),
            jax.ShapeDtypeStruct(second_moment.shape, f32),
        ),
        in_specs=[
            pl.BlockSpec((rows * 8, rank), lambda j: (0, 0)),
            pl.BlockSpec((1, rank, cols), lambda j: (j, 0, 0)),
            pl.BlockSpec((own, cols), lambda j: (0, j)),
            pl.BlockSpec((own, cols), lambda j: (0, j)),
        ],
        out_specs=(
            pl.BlockSpec((rows * 8, cols), lambda j: (0, j)),
            pl.BlockSpec((own, cols), lambda j: (0, j)),
            pl.BlockSpec((own, cols), lambda j: (0, j)),
        ),
        name="decode",
    )(basis, norm, nf, ns)


def solution(mesh):
    in_specs = (
        P("dp", None),
        P("dp", "tensor"),
        P(("dp", "tensor"), None),
        P("dp", "tensor"),
        P("dp", "tensor"),
    )
    out_specs = (P("dp", "tensor"), P("dp", "tensor"), P("dp", "tensor"))
    return jax.shard_map(
        per_device, mesh=mesh, in_specs=in_specs, out_specs=out_specs, check_vma=False
    )
```

time: 321 us -> 104 us (0.32)
  waiting for transfers between devices: 144 us -> 0 us
  Pallas kernels: 0 us -> 104 us
  blocking collectives: 95.4 us -> 0 us
  local copies, waits for them, and re-layouts: 35.9 us -> 0 us
  matrix products: 19.1 us -> 0 us
  between operations: 14.1 us -> 0.64 us
  starting transfers between devices: 9.53 us -> 0 us
    pallas_call x0 -> x2, Pallas kernels: none -> 104 us  [the longest x1 94.7 us: per_device(): pl.pallas_call(fused, out_shape=(jax.ShapeDtypeStruct((CHUNKS, rank, cols...]
    reduce_scatter x1 -> x0, waiting for transfers between devices: 101 us -> none  [per_device(): lax.psum_scatter(lax.dot_general(projected, out_grad, (((0,), (0,)), ((),...]
    psum x1 -> x0, blocking collectives: 84.2 us -> none  [per_device(): projected = lax.psum(partial_sum, 'tensor')]
    all_gather x1 -> x0, waiting for transfers between devices: 42.9 us -> none  [per_device(): lax.all_gather(normalized, 'dp', axis=0, tiled=True)]
    unnamed x8 -> x0, local copies, waits for them, and re-layouts: 30.8 us -> none
    dot_general x3 -> x0, matrix products: 19.1 us -> none  [the longest x1 9.15 us: per_device(): lax.dot_general(projected, out_grad, (((0,), (0,)), ((), ())), preferred_...]
    all_to_all x1 -> x0, blocking collectives: 11.2 us -> none  [sent_to_all(): return lax.all_to_all(copies, axis, split_axis=0, concat_axis=0, tiled=True)]
    all_to_all x1 -> x0, starting transfers between devices: 9.45 us -> none  [sent_to_all(): return lax.all_to_all(copies, axis, split_axis=0, concat_axis=0, tiled=True)]
  transfers between devices with their start and end apart: 3 -> 0, of which waited for: 2 -> 0; matrix products, arithmetic and copies ran while one was open for 8% -> 0% of each run, Pallas kernels for 0% -> 0%
where the time goes in v1:
time: 104 us
  Pallas kernels  104 us (100%)
    pallas_call x1, Pallas kernels, per_device(): pl.pallas_call(fused, out_shape=(jax.ShapeDtypeStruct((CHUNKS, rank, cols...  94.7 us
    pallas_call x1, Pallas kernels, per_device(): pl.pallas_call(decode, grid=(CHUNKS,), out_shape=(jax.ShapeDtypeStruct((r...  8.85 us

profile of v1, /device:TPU:1, one launch (start us, length us, event | category | flops | bytes accessed | tf_op | source)
XLA Modules:
  0.0 104.2 jit_solution(13886348226930444107)
XLA Ops:
  0.6 94.7 %fused.1 = (bf16[7,512,512]{2,1,0:T(8,128)(2,1)}, bf16[512,512]{1,0:T(8,128)(2,1)}, f32[32,3584]{1,0:T(8,128)}, f32[32,3584]{1,0:T(8,128)}) custom-call(bf16[1024,8192]{1,0:T(8,128)(2,1)} %act_hbm.1, bf16[1024,3584]{1,0:T(8,128)(2,1)} %grad_hbm.1, bf16[64,512]{1,0:T(8,128)(2,1)} %proj_ref.1, f32[32,3584]{1,0:T(8,128)} %first_ref.1, f32[32,3584]{1,0:T(8,128)} %second_ref.1), custom_call_target="tpu_custom_call" | custom-call | tf_op jit(solution)/shard_map/fused/pallas_call | solution.py:280
  95.3 8.9 %decode.1 = (f32[512,3584]{1,0:T(8,128)}, f32[32,3584]{1,0:T(8,128)}, f32[32,3584]{1,0:T(8,128)}) custom-call(bf16[512,512]{1,0:T(8,128)(2,1)} %get-tuple-element.7.basis_ref, bf16[7,512,512]{2,1,0:T(8,128)(2,1)} %get-tuple-element.8.norm_ref, f32[32,3584]{1,0:T(8,128)} %get-tuple-element.9.nf_ref, f32[32,3584]{1,0:T(8,128)} %get-tuple-element.10.ns_ref), custom_call_target="tpu_custom_call" | custom-call | tf_op jit(solution)/shard_map/decode/pallas_call | solution.py:311

commit v2 on v0

v2 whole, which is shorter than its diff:
```python
import jax
import jax.numpy as jnp
from jax import lax
from jax.experimental import pallas as pl
from jax.experimental.pallas import tpu as pltpu
from jax.sharding import PartitionSpec as P

beta_one = 0.9
beta_two = 0.999
bias_one = 1.0 - 0.9**10
bias_two = 1.0 - 0.999**10
adam_eps = 1e-08

MESH = pl.DeviceIdType.MESH
CHUNKS = 4
UNITS = 2 * CHUNKS
STEP = 256
LAGS = (2, 2, 0, 2, 4)
SLOTS = 3
NT = (((1,), (1,)), ((), ()))


def fused(act_hbm, grad_hbm, proj_hbm, first_hbm, second_hbm,
          norm, basis, nfirst, nsecond,
          act, grad, proj, part, first, second, slices, acc, pj, res, th_in, out1, in1, out2, in2,
          act_sem, grad_sem, local_sem, sent_sem, once_sem,
          b_r, f_r, c_r, t_r, p_r, q_r, g_r, h_r):
    dp = lax.axis_index("dp")
    tn = lax.axis_index("tensor")
    chip, core = dp // 2, dp % 2
    yh, zz = chip // 4, chip % 4
    rows = proj.shape[0]
    width = act.shape[2]
    cols = grad.shape[2]
    own = first.shape[0] // 2

    def chip_to(i):
        return ((yh + i // 4) % 2) * 4 + (zz + i % 4) % 4

    def chip_from(i):
        return ((yh + i // 4) % 2) * 4 + (zz + 4 - i % 4) % 4

    def tensor_to(i):
        return ((tn // 2 + i // 2) % 4) * 2 + (tn % 2 + i % 2) % 2

    def tensor_from(i):
        return ((tn // 2 + 4 - i // 2) % 4) * 2 + (tn % 2 + i % 2) % 2

    def at_chip(i):
        return {"dp": chip_to(i) * 2 + core}

    partner = {"dp": chip * 2 + (1 - core)}

    def remote(src, dst, send, recv, to):
        return pltpu.make_async_remote_copy(src, dst, send, recv, device_id=to, device_id_type=MESH)

    def arrive(ref, sem):
        pltpu.make_async_copy(ref, ref, sem).wait()

    a_s, b_s, f_s, c_s, e_s, t_s, p_s, d_s = (sent_sem.at[i] for i in range(8))
    a_r, e_r, n_s, n_r, d_r = (once_sem.at[i] for i in range(5))

    def act_copy(k):
        return pltpu.make_async_copy(
            act_hbm.at[:, pl.ds(pl.multiple_of(k * width, 128), width)], act.at[k], act_sem.at[k])

    def grad_copy(j):
        return pltpu.make_async_copy(
            grad_hbm.at[:, pl.ds(pl.multiple_of(j * cols, 128), cols)], grad.at[j], grad_sem)

    barrier = pltpu.get_barrier_semaphore()
    for i in range(1, 8):
        pl.semaphore_signal(barrier, inc=1, device_id={"tensor": tensor_to(i)}, device_id_type=MESH)
        pl.semaphore_signal(barrier, inc=1, device_id=at_chip(i), device_id_type=MESH)
    pl.semaphore_signal(barrier, inc=1, device_id=partner, device_id_type=MESH)

    proj_copy = pltpu.make_async_copy(proj_hbm, proj, local_sem.at[0])
    first_copy = pltpu.make_async_copy(first_hbm, first, local_sem.at[1])
    second_copy = pltpu.make_async_copy(second_hbm, second, local_sem.at[2])
    proj_copy.start()
    my_rows = pl.ds(pl.multiple_of(tn * rows, 16), rows)
    proj_copy.wait()
    for c in (core, 1 - core):
        act_copy(chip * 2 + c).start()
    for i in range(1, 8):
        for c in (core, 1 - core):
            act_copy(chip_from(i) * 2 + c).start()
    for j in range(CHUNKS):
        grad_copy(j).start()
    first_copy.start()
    second_copy.start()

    with jax.named_scope("barrier_wait"):
        pl.semaphore_wait(barrier, 15)

    def lanes(t):
        return pl.ds(pl.multiple_of((t // 2) * 128, 128), 128)

    def a_copy(i):
        return remote(proj.at[:, lanes(tensor_to(i))], part.at[my_rows], a_s, a_r,
                      {"tensor": tensor_to(i)})

    e_near = remote(proj, basis.at[my_rows], n_s, n_r, {"tensor": tensor_to(1)})

    def e_copy(i, x):
        there = pl.ds(pl.multiple_of(x * 2 * rows, 16), 2 * rows)
        return remote(basis.at[there], basis.at[there], e_s, e_r, {"tensor": tensor_to(2 * i)})

    for i in range(1, 8):
        a_copy(i).start()
    e_near.start()
    part[my_rows] = proj[:, lanes(tn)]
    basis[my_rows] = proj[...]
    ranks = slices.shape[1]
    pick = (lax.broadcasted_iota(jnp.int32, (ranks, 128), 1)
            == lax.broadcasted_iota(jnp.int32, (ranks, 128), 0) + (tn % 2) * ranks)
    pick = jnp.where(pick, 1.0, 0.0).astype(jnp.bfloat16)
    with jax.named_scope("a_wait"):
        arrive(part.at[0:7 * rows], a_r)

    slices[dp] = lax.dot_general(
        pick, part[...], NT, preferred_element_type=jnp.float32).astype(jnp.bfloat16)

    def b_copy(i):
        return remote(slices.at[dp], slices.at[dp], b_s, b_r.at[i], at_chip(i))

    b_pair = remote(slices.at[dp], slices.at[dp], b_s, b_r.at[0], partner)

    def f_copy(i):
        src = chip_from(i) * 2 + core
        return remote(slices.at[src], slices.at[src], f_s, f_r.at[i], partner)

    for i in range(1, 8):
        b_copy(i).start()
    b_pair.start()

    def product(k):
        act_copy(k).wait()
        return lax.dot_general(act[k], slices[k], NT, preferred_element_type=jnp.float32)

    def project(k):
        acc[...] += product(k)

    with jax.named_scope("near"):
        acc[...] = product(dp)
        b_pair.wait_recv()
        project(chip * 2 + (1 - core))

    def arrived(i, _):
        @pl.when(i < 8)
        def _():
            b_copy(i).wait_recv()
            f_copy(i).start()
            project(chip_from(i) * 2 + core)

        @pl.when(i > 1)
        def _():
            f_copy(i - 1).wait_recv()
            project(chip_from(i - 1) * 2 + (1 - core))
        return 0

    with jax.named_scope("arrived"):
        lax.fori_loop(1, 9, arrived, 0)

    def block(t):
        return pl.ds(pl.multiple_of(t * own, 16), own)

    done = acc[...].T.astype(jnp.bfloat16)
    for c in range(2):
        for u in range(2):
            pj[u, c, block(tn)] = done[(2 * c + u) * own:(2 * c + u + 1) * own]

    def c_copy(u, i, t):
        return remote(pj.at[u, :, block(t)], pj.at[u, :, block(t)], c_s, c_r.at[u],
                      {"tensor": tensor_to(i)})

    def c_wait(u):
        arrive(pj.at[u, :, 0:7 * own], c_r.at[u])

    for u in range(2):
        for i in range(1, 8):
            c_copy(u, i, tn).start()
    arrive(grad, grad_sem)
    e_near.wait_recv()
    for i in range(1, 4):
        e_copy(i, tn // 2).start()

    def t_copy(n):
        return remote(res.at[n, 1 - core], th_in.at[n], t_s, t_r.at[n], partner)

    def dots(n):
        left = pj[n // CHUNKS].reshape(16 * own, acc.shape[0])
        for s in range(0, cols, STEP):
            w = min(STEP, cols - s)
            res[n, :, :, :, :, s:s + w] = jnp.dot(
                left, grad[n % CHUNKS, :, s:s + w], preferred_element_type=jnp.float32
            ).reshape(2, 2, 4, own, w)
        t_copy(n).start()

    def p_y(j):
        return remote(out1.at[j, 1 - yh], in1.at[j, :, 0], p_s, p_r.at[j], at_chip(4))

    def p_z(j, i):
        return remote(out1.at[j, :, (zz + i) % 4], in1.at[j, i], p_s, p_r.at[j], at_chip(i))

    def q_z(j, i):
        return remote(out2.at[j, (zz + i) % 4], in2.at[j, i], p_s, q_r.at[j], at_chip(i))

    def q_y(j):
        return remote(out2.at[j, 1 - yh], in2.at[j, 0], p_s, q_r.at[j], at_chip(4))

    def g_z(j, i, z):
        return remote(norm.at[j, core, yh, z], norm.at[j, core, yh, z], p_s, g_r.at[j], at_chip(i))

    def g_y(j, y):
        return remote(norm.at[j, core, y, zz], norm.at[j, core, y, zz], p_s, g_r.at[j], at_chip(4))

    def h_y(j, y):
        return remote(norm.at[j, core, y], norm.at[j, core, y], p_s, h_r.at[j], at_chip(4))

    def h_z(j, i, z):
        return remote(norm.at[j, core, :, z], norm.at[j, core, :, z], p_s, h_r.at[j], at_chip(i))

    def d_copy(j, c):
        return remote(norm.at[j, c], norm.at[j, c], d_s, d_r, partner)

    def y_first(n):
        return pl.when(n % 2 == 1)

    def z_first(n):
        return pl.when(n % 2 == 0)

    def combine(n):
        t_copy(n).wait_recv()

        @y_first(n)
        def _():
            out1[n, 1 - yh] = (res[n, core, 1 - yh] + th_in[n, 1 - yh]).astype(jnp.bfloat16)
            p_y(n).start()

        @z_first(n)
        def _():
            for i in range(1, 4):
                z = (zz + i) % 4
                out1[n, :, z] = (res[n, core, :, z] + th_in[n, :, z]).astype(jnp.bfloat16)
                p_z(n, i).start()

    def stage_one(j):
        @y_first(j)
        def _():
            p_y(j).wait_recv()
            total = res[j, core, yh] + th_in[j, yh] + in1[j, :, 0].astype(jnp.float32)
            res[j, core, yh] = total
            out2[j] = total.astype(jnp.bfloat16)
            for i in range(1, 4):
                q_z(j, i).start()

        @z_first(j)
        def _():
            total = res[j, core, :, zz] + th_in[j, :, zz]
            arrive(in1.at[j, 1:4], p_r.at[j])
            for i in range(1, 4):
                total += in1[j, i].astype(jnp.float32)
            res[j, core, :, zz] = total
            out2[j, 0:2] = total.astype(jnp.bfloat16)
            q_y(j).start()

    def adam(j):
        @y_first(j)
        def _():
            total = res[j, core, yh, zz]
            arrive(in2.at[j, 1:4], q_r.at[j])
            for i in range(1, 4):
                total += in2[j, i].astype(jnp.float32)
            res[j, core, yh, zz] = total

        @z_first(j)
        def _():
            q_y(j).wait_recv()
            res[j, core, yh, zz] = res[j, core, yh, zz] + in2[j, 0].astype(jnp.float32)

        total = res[j, core, yh, zz]
        at = (pl.ds(pl.multiple_of((j // CHUNKS) * own, 8), own),
              pl.ds(pl.multiple_of((j % CHUNKS) * cols, 128), cols))
        new_first = beta_one * first[at] + (1.0 - beta_one) * total
        new_second = beta_two * second[at] + (1.0 - beta_two) * total * total
        nfirst[at] = new_first
        nsecond[at] = new_second
        norm[j, core, yh, zz] = (
            new_first / bias_one / (jnp.sqrt(new_second / bias_two) + adam_eps)).astype(jnp.bfloat16)

        @y_first(j)
        def _():
            for i in range(1, 4):
                g_z(j, i, zz).start()

        @z_first(j)
        def _():
            g_y(j, yh).start()

    def stage_two(j):
        @y_first(j)
        def _():
            arrive(norm.at[j, core, yh, 0:3], g_r.at[j])
            h_y(j, yh).start()

        @z_first(j)
        def _():
            g_y(j, 1 - yh).wait_recv()
            for i in range(1, 4):
                h_z(j, i, zz).start()

    def to_pair(j):
        @y_first(j)
        def _():
            h_y(j, 1 - yh).wait_recv()

        @z_first(j)
        def _():
            arrive(norm.at[j, core, :, 0:3], h_r.at[j])

        d_copy(j, core).start()

    def loop(steps, *stages):
        def body(k, _):
            for name, do, lag, first_unit, count in stages:
                @pl.when(jnp.logical_and(k >= lag, k < lag + count))
                def _():
                    with jax.named_scope(name):
                        do(first_unit + k - lag)
            return 0

        lax.fori_loop(0, steps, body, 0)

    with jax.named_scope("c_wait0"):
        c_wait(0)
    loop(CHUNKS + LAGS[0], ("dots", dots, 0, 0, CHUNKS), ("combine", combine, LAGS[0], 0, CHUNKS))
    with jax.named_scope("c_wait1"):
        c_wait(1)
    loop(CHUNKS + max(LAGS[:2]), ("dots", dots, 0, CHUNKS, CHUNKS), ("combine", combine, LAGS[0], CHUNKS, CHUNKS),
         ("one", stage_one, LAGS[1], 0, CHUNKS))
    first_copy.wait()
    second_copy.wait()
    loop(UNITS + LAGS[4], ("one", stage_one, 0, CHUNKS, CHUNKS), ("adam", adam, LAGS[2], 0, UNITS),
         ("two", stage_two, LAGS[3], 0, UNITS), ("pair", to_pair, LAGS[4], 0, UNITS))

    with jax.named_scope("finish"):
        arrive(part.at[0:7 * rows], a_s)
        arrive(slices.at[0:8], b_s)
        arrive(slices.at[0:7], f_s)
        arrive(pj.at[:, :, 0:7 * own], c_s)
        e_near.wait_send()
        arrive(basis.at[0:6 * rows], e_s)
        arrive(basis.at[0:6 * rows], e_r)
        arrive(res.at[:, 0], t_s)
        arrive(norm.at[0:UNITS * 14 // 16], p_s)
        arrive(norm.at[:, 0], d_s)
        arrive(norm.at[:, 0], d_r)


def decode(basis, norm, nf, ns, update, nf_out, ns_out, buf, sem, small_sem):
    cols = norm.shape[5]
    nf_copy = pltpu.make_async_copy(nf, nf_out, small_sem.at[0])
    ns_copy = pltpu.make_async_copy(ns, ns_out, small_sem.at[1])

    def out_copy(j):
        return pltpu.make_async_copy(
            buf.at[j % SLOTS], update.at[:, pl.ds(pl.multiple_of(j * cols, 128), cols)], sem.at[j % SLOTS])

    def step(j, _):
        @pl.when(j >= SLOTS)
        def _():
            out_copy(j - SLOTS).wait()
        block = jnp.concatenate(
            [norm[u * CHUNKS + j, c, y, z]
             for y in range(2) for z in range(4) for c in range(2) for u in range(2)], axis=0)
        buf[j % SLOTS] = jnp.dot(basis[...], block, preferred_element_type=jnp.float32)
        out_copy(j).start()
        return 0

    lax.fori_loop(0, CHUNKS, step, 0)
    nf_copy.start()
    ns_copy.start()
    for j in range(CHUNKS - SLOTS, CHUNKS):
        out_copy(j).wait()
    nf_copy.wait()
    ns_copy.wait()


def per_device(activations, out_grad, projector, first_moment, second_moment):
    tokens, width = activations.shape
    ff = out_grad.shape[1]
    rows, rank = projector.shape
    own = first_moment.shape[0] // 2
    cols = ff // CHUNKS
    half = rank // 2
    bf, f32 = jnp.bfloat16, jnp.float32
    vmem = pl.BlockSpec(memory_space=pltpu.VMEM)
    any_ = pl.BlockSpec(memory_space=pl.ANY)
    dma = pltpu.SemaphoreType.DMA
    norm, basis, nf, ns = pl.pallas_call(
        fused,
        out_shape=(
            pltpu.VMEM((UNITS, 2, 2, 4, own, cols), bf),
            pltpu.VMEM((rows * 8, rank), bf),
            pltpu.VMEM(first_moment.shape, f32),
            pltpu.VMEM(second_moment.shape, f32),
        ),
        in_specs=[any_] * 5,
        out_specs=(vmem, vmem, vmem, vmem),
        scratch_shapes=[
            pltpu.VMEM((16, tokens, width // 16), bf),
            pltpu.VMEM((CHUNKS, tokens, cols), bf),
            pltpu.VMEM((rows, rank), bf),
            pltpu.VMEM((rows * 8, 128), bf),
            pltpu.VMEM(first_moment.shape, f32),
            pltpu.VMEM(second_moment.shape, f32),
            pltpu.VMEM((16, rank // 8, width // 16), bf),
            pltpu.VMEM((tokens, rank // 8), f32),
            pltpu.VMEM((2, 2, half // 2, tokens), bf),
            pltpu.VMEM((UNITS, 2, 2, 4, own, cols), f32),
            pltpu.VMEM((UNITS, 2, 4, own, cols), f32),
            pltpu.VMEM((UNITS, 2, 4, own, cols), bf),
            pltpu.VMEM((UNITS, 4, 2, own, cols), bf),
            pltpu.VMEM((UNITS, 4, own, cols), bf),
            pltpu.VMEM((UNITS, 4, own, cols), bf),
            dma((16,)), dma, dma((3,)), dma((8,)), dma((5,)),
            dma((8,)), dma((8,)), dma((2,)), dma((UNITS,)),
            dma((UNITS,)), dma((UNITS,)), dma((UNITS,)), dma((UNITS,)),
        ],
        compiler_params=pltpu.CompilerParams(
            collective_id=0, has_side_effects=True, vmem_limit_bytes=54 * 2**20),
        name="fused",
    )(activations, out_grad, projector, first_moment, second_moment)
    return pl.pallas_call(
        decode,
        out_shape=(
            jax.ShapeDtypeStruct((rows * 8, ff), f32),
            jax.ShapeDtypeStruct(first_moment.shape, f32),
            jax.ShapeDtypeStruct(second_moment.shape, f32),
        ),
        in_specs=[vmem] * 4,
        out_specs=(any_, any_, any_),
        scratch_shapes=[
            pltpu.VMEM((SLOTS, rows * 8, cols), f32),
            dma((SLOTS,)), dma((2,)),
        ],
        compiler_params=pltpu.CompilerParams(vmem_limit_bytes=16 * 2**20),
        name="decode",
    )(basis, norm, nf, ns)


def solution(mesh):
    in_specs = (
        P("dp", None),
        P("dp", "tensor"),
        P(("dp", "tensor"), None),
        P("dp", "tensor"),
        P("dp", "tensor"),
    )
    out_specs = (P("dp", "tensor"), P("dp", "tensor"), P("dp", "tensor"))
    return jax.shard_map(
        per_device, mesh=mesh, in_specs=in_specs, out_specs=out_specs, check_vma=False
    )
```

time: 321 us -> 82.9 us (0.26)
  waiting for transfers between devices: 144 us -> 0 us
  blocking collectives: 95.4 us -> 0 us
  Pallas kernels: 0 us -> 81.1 us
  local copies, waits for them, and re-layouts: 35.9 us -> 0 us
  matrix products: 19.1 us -> 0 us
  between operations: 14.1 us -> 0.64 us
  starting transfers between devices: 9.53 us -> 0 us
    reduce_scatter x1 -> x0, waiting for transfers between devices: 101 us -> none  [per_device(): lax.psum_scatter(lax.dot_general(projected, out_grad, (((0,), (0,)), ((),...]
    psum x1 -> x0, blocking collectives: 84.2 us -> none  [per_device(): projected = lax.psum(partial_sum, 'tensor')]
    pallas_call x0 -> x2, Pallas kernels: none -> 81.1 us  [the longest x1 76.8 us: per_device(): pl.pallas_call(fused, out_shape=(pltpu.VMEM((UNITS, 2, 2, 4, own, cols),...]
    all_gather x1 -> x0, waiting for transfers between devices: 42.9 us -> none  [per_device(): lax.all_gather(normalized, 'dp', axis=0, tiled=True)]
    unnamed x8 -> x0, local copies, waits for them, and re-layouts: 30.8 us -> none
    dot_general x3 -> x0, matrix products: 19.1 us -> none  [the longest x1 9.15 us: per_device(): lax.dot_general(projected, out_grad, (((0,), (0,)), ((), ())), preferred_...]
    all_to_all x1 -> x0, blocking collectives: 11.2 us -> none  [sent_to_all(): return lax.all_to_all(copies, axis, split_axis=0, concat_axis=0, tiled=True)]
    all_to_all x1 -> x0, starting transfers between devices: 9.45 us -> none  [sent_to_all(): return lax.all_to_all(copies, axis, split_axis=0, concat_axis=0, tiled=True)]
  transfers between devices with their start and end apart: 3 -> 0, of which waited for: 2 -> 0; matrix products, arithmetic and copies ran while one was open for 8% -> 0% of each run, Pallas kernels for 0% -> 0%
where the time goes in v2:
time: 82.9 us; the launch traced here: 81.7 us
  Pallas kernels  81.1 us (98%)
    pallas_call x1, Pallas kernels, per_device(): pl.pallas_call(fused, out_shape=(pltpu.VMEM((UNITS, 2, 2, 4, own, cols),...  76.8 us
    pallas_call x1, Pallas kernels, per_device(): pl.pallas_call(decode, out_shape=(jax.ShapeDtypeStruct((rows * 8, ff), f3...  4.26 us

profile of v2, /device:TPU:1, one launch (start us, length us, event | category | flops | bytes accessed | tf_op | source)
XLA Modules:
  0.0 81.7 jit_solution(6948719624694882159)
XLA Ops:
  0.6 76.8 %fused.1 = (bf16[8,2,2,4,16,896]{5,4,3,2,1,0:T(8,128)(2,1)S(1)}, bf16[512,512]{1,0:T(8,128)(2,1)S(1)}, f32[32,3584]{1,0:T(8,128)S(1)}, f32[32,3584]{1,0:T(8,128)S(1)}) custom-call(bf16[1024,8192]{1,0:T(8,128)(2,1)} %act_hbm.1, bf16[1024,3584]{1,0:T(8,128)(2,1)} %grad_hbm.1, bf16[64,512]{1,0:T(8,128)(2,1)} %proj_hbm.1, f32[32,3584]{1,0:T(8,128)} %first_hbm.1, ...), custom_call_target="tpu_custom_call" | custom-call | tf_op jit(solution)/shard_map/fused/pallas_call | solution.py:401
  77.4 4.3 %decode.1 = (f32[512,3584]{1,0:T(8,128)}, f32[32,3584]{1,0:T(8,128)}, f32[32,3584]{1,0:T(8,128)}) custom-call(bf16[512,512]{1,0:T(8,128)(2,1)S(1)} %get-tuple-element.7.basis, bf16[8,2,2,4,16,896]{5,4,3,2,1,0:T(8,128)(2,1)S(1)} %get-tuple-element.8.norm, f32[32,3584]{1,0:T(8,128)S(1)} %get-tuple-element.9.nf, f32[32,3584]{1,0:T(8,128)S(1)} %get-tuple-element.10.ns), custom_call_target="tpu_custom_call" | custom-call | tf_op jit(solution)/shard_map/decode/pallas_call | solution.py:435

commit v3 on v2

--- a/solution.py
+++ b/solution.py
@@ -12,17 +12,20 @@
 adam_eps = 1e-08
 
 MESH = pl.DeviceIdType.MESH
-CHUNKS = 4
+CHUNKS = 7
+CHIP_ORDER = (1, 3, 4, 5, 7, 2, 6)
+TENSOR_ORDER = (5, 3, 7, 4, 2, 6, 1)
+Z_ORDER = (1, 2, 3)
 UNITS = 2 * CHUNKS
 STEP = 256
-LAGS = (2, 2, 0, 2, 4)
+LAGS = (2, 3, 0, 6, 11)
 SLOTS = 3
 NT = (((1,), (1,)), ((), ()))
 
 
 def fused(act_hbm, grad_hbm, proj_hbm, first_hbm, second_hbm,
           norm, basis, nfirst, nsecond,
-          act, grad, proj, part, first, second, slices, acc, pj, res, th_in, out1, in1, out2, in2,
+          act, grad, proj, part, first, second, slices, acc, pj, res, th_in, out1, in1, out2, in2, total_sent,
           act_sem, grad_sem, local_sem, sent_sem, once_sem,
           b_r, f_r, c_r, t_r, p_r, q_r, g_r, h_r):
     dp = lax.axis_index("dp")
@@ -69,9 +72,9 @@
             grad_hbm.at[:, pl.ds(pl.multiple_of(j * cols, 128), cols)], grad.at[j], grad_sem)
 
     barrier = pltpu.get_barrier_semaphore()
-    for i in range(1, 8):
-        pl.semaphore_signal(barrier, inc=1, device_id={"tensor": tensor_to(i)}, device_id_type=MESH)
+    for i, k in zip(CHIP_ORDER, TENSOR_ORDER):
         pl.semaphore_signal(barrier, inc=1, device_id=at_chip(i), device_id_type=MESH)
+        pl.semaphore_signal(barrier, inc=1, device_id={"tensor": tensor_to(k)}, device_id_type=MESH)
     pl.semaphore_signal(barrier, inc=1, device_id=partner, device_id_type=MESH)
 
     proj_copy = pltpu.make_async_copy(proj_hbm, proj, local_sem.at[0])
@@ -82,7 +85,7 @@
     proj_copy.wait()
     for c in (core, 1 - core):
         act_copy(chip * 2 + c).start()
-    for i in range(1, 8):
+    for i in CHIP_ORDER:
         for c in (core, 1 - core):
             act_copy(chip_from(i) * 2 + c).start()
     for j in range(CHUNKS):
@@ -106,7 +109,7 @@
         there = pl.ds(pl.multiple_of(x * 2 * rows, 16), 2 * rows)
         return remote(basis.at[there], basis.at[there], e_s, e_r, {"tensor": tensor_to(2 * i)})
 
-    for i in range(1, 8):
+    for i in TENSOR_ORDER:
         a_copy(i).start()
     e_near.start()
     part[my_rows] = proj[:, lanes(tn)]
@@ -130,13 +133,13 @@
         src = chip_from(i) * 2 + core
         return remote(slices.at[src], slices.at[src], f_s, f_r.at[i], partner)
 
-    for i in range(1, 8):
+    for i in CHIP_ORDER:
         b_copy(i).start()
     b_pair.start()
 
     def product(k):
         act_copy(k).wait()
-        return lax.dot_general(act[k], slices[k], NT, preferred_element_type=jnp.float32)
+        return lax.dot_general(slices[k], act[k], NT, preferred_element_type=jnp.float32)
 
     def project(k):
         acc[...] += product(k)
@@ -146,54 +149,65 @@
         b_pair.wait_recv()
         project(chip * 2 + (1 - core))
 
-    def arrived(i, _):
-        @pl.when(i < 8)
-        def _():
-            b_copy(i).wait_recv()
-            f_copy(i).start()
-            project(chip_from(i) * 2 + core)
-
-        @pl.when(i > 1)
-        def _():
-            f_copy(i - 1).wait_recv()
-            project(chip_from(i - 1) * 2 + (1 - core))
-        return 0
-
     with jax.named_scope("arrived"):
-        lax.fori_loop(1, 9, arrived, 0)
+        for i, before in zip(CHIP_ORDER + (None,), (None,) + CHIP_ORDER):
+            if i is not None:
+                b_copy(i).wait_recv()
+                f_copy(i).start()
+                project(chip_from(i) * 2 + core)
+            if before is not None:
+                f_copy(before).wait_recv()
+                project(chip_from(before) * 2 + (1 - core))
 
     def block(t):
         return pl.ds(pl.multiple_of(t * own, 16), own)
 
-    done = acc[...].T.astype(jnp.bfloat16)
+    done = acc[...].astype(jnp.bfloat16)
     for c in range(2):
         for u in range(2):
             pj[u, c, block(tn)] = done[(2 * c + u) * own:(2 * c + u + 1) * own]
 
-    def c_copy(u, i, t):
-        return remote(pj.at[u, :, block(t)], pj.at[u, :, block(t)], c_s, c_r.at[u],
+    def c_copy(i):
+        return remote(pj.at[1, :, block(tn)], pj.at[1, :, block(tn)], c_s, c_r.at[2],
                       {"tensor": tensor_to(i)})
 
-    def c_wait(u):
-        arrive(pj.at[u, :, 0:7 * own], c_r.at[u])
-
-    for u in range(2):
+    def c_half(side, i, k):
+        return remote(pj.at[0, side, block(tn)], pj.at[0, side, block(tn)], c_s, c_r.at[k],
+                      {"tensor": tensor_to(i)})
+
+    for k, side in ((0, 1 - core), (1, core)):
         for i in range(1, 8):
-            c_copy(u, i, tn).start()
+            c_half(side, i, k).start()
+    for i in range(1, 8):
+        c_copy(i).start()
     arrive(grad, grad_sem)
     e_near.wait_recv()
-    for i in range(1, 4):
+    for i in Z_ORDER:
         e_copy(i, tn // 2).start()
 
     def t_copy(n):
         return remote(res.at[n, 1 - core], th_in.at[n], t_s, t_r.at[n], partner)
 
+    def half_dots(n, side):
+        for s in range(0, cols, STEP):
+            w = min(STEP, cols - s)
+            res[n, side, :, :, :, s:s + w] = jnp.dot(
+                pj[0, side], grad[n, :, s:s + w], preferred_element_type=jnp.float32
+            ).reshape(2, 4, own, w)
+
+    def theirs(n):
+        half_dots(n, 1 - core)
+        t_copy(n).start()
+
+    def mine(n):
+        half_dots(n, core)
+
     def dots(n):
-        left = pj[n // CHUNKS].reshape(16 * own, acc.shape[0])
+        left = pj[1].reshape(16 * own, acc.shape[1])
         for s in range(0, cols, STEP):
             w = min(STEP, cols - s)
             res[n, :, :, :, :, s:s + w] = jnp.dot(
-                left, grad[n % CHUNKS, :, s:s + w], preferred_element_type=jnp.float32
+                left, grad[n - CHUNKS, :, s:s + w], preferred_element_type=jnp.float32
             ).reshape(2, 2, 4, own, w)
         t_copy(n).start()
 
@@ -224,11 +238,23 @@
     def d_copy(j, c):
         return remote(norm.at[j, c], norm.at[j, c], d_s, d_r, partner)
 
+    def reduce_z(n):
+        return n % 2 == 0
+
+    def gather_y(n):
+        return n % 2 == 1
+
     def y_first(n):
-        return pl.when(n % 2 == 1)
+        return pl.when(jnp.logical_not(reduce_z(n)))
 
     def z_first(n):
-        return pl.when(n % 2 == 0)
+        return pl.when(reduce_z(n))
+
+    def then_y(n):
+        return pl.when(jnp.logical_not(gather_y(n)))
+
+    def then_z(n):
+        return pl.when(gather_y(n))
 
     def combine(n):
         t_copy(n).wait_recv()
@@ -240,7 +266,7 @@
 
         @z_first(n)
         def _():
-            for i in range(1, 4):
+            for i in Z_ORDER:
                 z = (zz + i) % 4
                 out1[n, :, z] = (res[n, core, :, z] + th_in[n, :, z]).astype(jnp.bfloat16)
                 p_z(n, i).start()
@@ -252,7 +278,7 @@
             total = res[j, core, yh] + th_in[j, yh] + in1[j, :, 0].astype(jnp.float32)
             res[j, core, yh] = total
             out2[j] = total.astype(jnp.bfloat16)
-            for i in range(1, 4):
+            for i in Z_ORDER:
                 q_z(j, i).start()
 
         @z_first(j)
@@ -289,33 +315,33 @@
         norm[j, core, yh, zz] = (
             new_first / bias_one / (jnp.sqrt(new_second / bias_two) + adam_eps)).astype(jnp.bfloat16)
 
-        @y_first(j)
-        def _():
-            for i in range(1, 4):
+        @then_y(j)
+        def _():
+            for i in Z_ORDER:
                 g_z(j, i, zz).start()
 
-        @z_first(j)
+        @then_z(j)
         def _():
             g_y(j, yh).start()
 
     def stage_two(j):
-        @y_first(j)
+        @then_y(j)
         def _():
             arrive(norm.at[j, core, yh, 0:3], g_r.at[j])
             h_y(j, yh).start()
 
-        @z_first(j)
+        @then_z(j)
         def _():
             g_y(j, 1 - yh).wait_recv()
-            for i in range(1, 4):
+            for i in Z_ORDER:
                 h_z(j, i, zz).start()
 
     def to_pair(j):
-        @y_first(j)
+        @then_y(j)
         def _():
             h_y(j, 1 - yh).wait_recv()
 
-        @z_first(j)
+        @then_z(j)
         def _():
             arrive(norm.at[j, core, :, 0:3], h_r.at[j])
 
@@ -333,10 +359,13 @@
         lax.fori_loop(0, steps, body, 0)
 
     with jax.named_scope("c_wait0"):
-        c_wait(0)
-    loop(CHUNKS + LAGS[0], ("dots", dots, 0, 0, CHUNKS), ("combine", combine, LAGS[0], 0, CHUNKS))
+        arrive(pj.at[0, 0, 0:7 * own], c_r.at[0])
+    loop(CHUNKS, ("theirs", theirs, 0, 0, CHUNKS))
     with jax.named_scope("c_wait1"):
-        c_wait(1)
+        arrive(pj.at[0, 0, 0:7 * own], c_r.at[1])
+    loop(CHUNKS, ("dots", mine, 0, 0, CHUNKS), ("combine", combine, 0, 0, CHUNKS))
+    with jax.named_scope("c_wait1"):
+        arrive(pj.at[1, :, 0:7 * own], c_r.at[2])
     loop(CHUNKS + max(LAGS[:2]), ("dots", dots, 0, CHUNKS, CHUNKS), ("combine", combine, LAGS[0], CHUNKS, CHUNKS),
          ("one", stage_one, LAGS[1], 0, CHUNKS))
     first_copy.wait()
@@ -353,7 +382,7 @@
         arrive(basis.at[0:6 * rows], e_s)
         arrive(basis.at[0:6 * rows], e_r)
         arrive(res.at[:, 0], t_s)
-        arrive(norm.at[0:UNITS * 14 // 16], p_s)
+        arrive(total_sent, p_s)
         arrive(norm.at[:, 0], d_s)
         arrive(norm.at[:, 0], d_r)
 
@@ -416,7 +445,7 @@
             pltpu.VMEM(first_moment.shape, f32),
             pltpu.VMEM(second_moment.shape, f32),
             pltpu.VMEM((16, rank // 8, width // 16), bf),
-            pltpu.VMEM((tokens, rank // 8), f32),
+            pltpu.VMEM((rank // 8, tokens), f32),
             pltpu.VMEM((2, 2, half // 2, tokens), bf),
             pltpu.VMEM((UNITS, 2, 2, 4, own, cols), f32),
             pltpu.VMEM((UNITS, 2, 4, own, cols), f32),
@@ -424,8 +453,9 @@
             pltpu.VMEM((UNITS, 4, 2, own, cols), bf),
             pltpu.VMEM((UNITS, 4, own, cols), bf),
             pltpu.VMEM((UNITS, 4, own, cols), bf),
+            pltpu.VMEM((UNITS, 14, own, cols), bf),
             dma((16,)), dma, dma((3,)), dma((8,)), dma((5,)),
-            dma((8,)), dma((8,)), dma((2,)), dma((UNITS,)),
+            dma((8,)), dma((8,)), dma((3,)), dma((UNITS,)),
             dma((UNITS,)), dma((UNITS,)), dma((UNITS,)), dma((UNITS,)),
         ],
         compiler_params=pltpu.CompilerParams(

time: 82.9 us -> 74.2 us (0.90); the launches traced: 81.7 us -> 74.1 us
  Pallas kernels: 81.1 us -> 73.4 us
    pallas_call x1, Pallas kernels: 76.8 us -> 69 us  [per_device(): pl.pallas_call(fused, out_shape=(pltpu.VMEM((UNITS, 2, 2, 4, own, cols),...]
where the time goes in v3:
time: 74.2 us; the launch traced here: 74.1 us
  Pallas kernels  73.4 us (99%)
    pallas_call x1, Pallas kernels, per_device(): pl.pallas_call(fused, out_shape=(pltpu.VMEM((UNITS, 2, 2, 4, own, cols),...  69 us
    pallas_call x1, Pallas kernels, per_device(): pl.pallas_call(decode, out_shape=(jax.ShapeDtypeStruct((rows * 8, ff), f3...  4.39 us

profile of v3, /device:TPU:1, one launch (start us, length us, event | category | flops | bytes accessed | tf_op | source)
XLA Modules:
  0.0 74.1 jit_solution(14281622288140070559)
XLA Ops:
  0.6 69.0 %fused.1 = (bf16[14,2,2,4,16,512]{5,4,3,2,1,0:T(8,128)(2,1)S(1)}, bf16[512,512]{1,0:T(8,128)(2,1)S(1)}, f32[32,3584]{1,0:T(8,128)S(1)}, f32[32,3584]{1,0:T(8,128)S(1)}) custom-call(bf16[1024,8192]{1,0:T(8,128)(2,1)} %act_hbm.1, bf16[1024,3584]{1,0:T(8,128)(2,1)} %grad_hbm.1, bf16[64,512]{1,0:T(8,128)(2,1)} %proj_hbm.1, f32[32,3584]{1,0:T(8,128)} %first_hbm.1, ...), custom_call_target="tpu_custom_call" | custom-call | tf_op jit(solution)/shard_map/fused/pallas_call | solution.py:430
  69.7 4.4 %decode.1 = (f32[512,3584]{1,0:T(8,128)}, f32[32,3584]{1,0:T(8,128)}, f32[32,3584]{1,0:T(8,128)}) custom-call(bf16[512,512]{1,0:T(8,128)(2,1)S(1)} %get-tuple-element.7.basis, bf16[14,2,2,4,16,512]{5,4,3,2,1,0:T(8,128)(2,1)S(1)} %get-tuple-element.8.norm, f32[32,3584]{1,0:T(8,128)S(1)} %get-tuple-element.9.nf, f32[32,3584]{1,0:T(8,128)S(1)} %get-tuple-element.10.ns), custom_call_target="tpu_custom_call" | custom-call | tf_op jit(solution)/shard_map/decode/pallas_call | solution.py:465

commit v4 on v3

--- a/solution.py
+++ b/solution.py
@@ -18,7 +18,7 @@
 Z_ORDER = (1, 2, 3)
 UNITS = 2 * CHUNKS
 STEP = 256
-LAGS = (2, 3, 0, 6, 11)
+LAGS = (2, 1, 0, 7, 13)
 SLOTS = 3
 NT = (((1,), (1,)), ((), ()))
 
@@ -114,72 +114,71 @@
     e_near.start()
     part[my_rows] = proj[:, lanes(tn)]
     basis[my_rows] = proj[...]
-    ranks = slices.shape[1]
-    pick = (lax.broadcasted_iota(jnp.int32, (ranks, 128), 1)
-            == lax.broadcasted_iota(jnp.int32, (ranks, 128), 0) + (tn % 2) * ranks)
-    pick = jnp.where(pick, 1.0, 0.0).astype(jnp.bfloat16)
+    ranks = 2 * slices.shape[2]
+    row = lax.broadcasted_iota(jnp.int32, (2, 2, own, 128), 2)
+    row += own * (lax.broadcasted_iota(jnp.int32, (2, 2, own, 128), 0)
+                  + 2 * lax.broadcasted_iota(jnp.int32, (2, 2, own, 128), 1))
+    pick = lax.broadcasted_iota(jnp.int32, (2, 2, own, 128), 3) == row + (tn % 2) * ranks
+    pick = jnp.where(pick, 1.0, 0.0).reshape(ranks, 128).astype(jnp.bfloat16)
     with jax.named_scope("a_wait"):
         arrive(part.at[0:7 * rows], a_r)
 
-    slices[dp] = lax.dot_general(
-        pick, part[...], NT, preferred_element_type=jnp.float32).astype(jnp.bfloat16)
-
-    def b_copy(i):
-        return remote(slices.at[dp], slices.at[dp], b_s, b_r.at[i], at_chip(i))
-
-    b_pair = remote(slices.at[dp], slices.at[dp], b_s, b_r.at[0], partner)
-
-    def f_copy(i):
+    both = lax.dot_general(pick, part[...], NT, preferred_element_type=jnp.float32).astype(jnp.bfloat16)
+    for u in range(2):
+        slices[u, dp] = both[u * ranks // 2:(u + 1) * ranks // 2]
+
+    def b_copy(u, i):
+        to = at_chip(i) if i else partner
+        return remote(slices.at[u, dp], slices.at[u, dp], b_s, b_r.at[u, i], to)
+
+    def f_copy(u, i):
         src = chip_from(i) * 2 + core
-        return remote(slices.at[src], slices.at[src], f_s, f_r.at[i], partner)
-
-    for i in CHIP_ORDER:
-        b_copy(i).start()
-    b_pair.start()
-
-    def product(k):
-        act_copy(k).wait()
-        return lax.dot_general(slices[k], act[k], NT, preferred_element_type=jnp.float32)
-
-    def project(k):
-        acc[...] += product(k)
-
-    with jax.named_scope("near"):
-        acc[...] = product(dp)
-        b_pair.wait_recv()
-        project(chip * 2 + (1 - core))
-
-    with jax.named_scope("arrived"):
-        for i, before in zip(CHIP_ORDER + (None,), (None,) + CHIP_ORDER):
-            if i is not None:
-                b_copy(i).wait_recv()
-                f_copy(i).start()
-                project(chip_from(i) * 2 + core)
-            if before is not None:
-                f_copy(before).wait_recv()
-                project(chip_from(before) * 2 + (1 - core))
+        return remote(slices.at[u, src], slices.at[u, src], f_s, f_r.at[u, i], partner)
+
+    for u in range(2):
+        for i in CHIP_ORDER + (0,):
+            b_copy(u, i).start()
+
+    def project_half(u):
+        def product(k):
+            if u == 0:
+                act_copy(k).wait()
+            return lax.dot_general(slices[u, k], act[k], NT, preferred_element_type=jnp.float32)
+
+        with jax.named_scope("near"):
+            acc[...] = product(dp)
+            b_copy(u, 0).wait_recv()
+            acc[...] += product(chip * 2 + (1 - core))
+
+        with jax.named_scope("arrived"):
+            for i, before in zip(CHIP_ORDER + (None,), (None,) + CHIP_ORDER):
+                if i is not None:
+                    b_copy(u, i).wait_recv()
+                    f_copy(u, i).start()
+                    acc[...] += product(chip_from(i) * 2 + core)
+                if before is not None:
+                    f_copy(u, before).wait_recv()
+                    acc[...] += product(chip_from(before) * 2 + (1 - core))
 
     def block(t):
         return pl.ds(pl.multiple_of(t * own, 16), own)
 
-    done = acc[...].astype(jnp.bfloat16)
-    for c in range(2):
-        for u in range(2):
-            pj[u, c, block(tn)] = done[(2 * c + u) * own:(2 * c + u + 1) * own]
-
-    def c_copy(i):
-        return remote(pj.at[1, :, block(tn)], pj.at[1, :, block(tn)], c_s, c_r.at[2],
+    def c_copy(u, side, i, k):
+        return remote(pj.at[u, side, block(tn)], pj.at[u, side, block(tn)], c_s, c_r.at[k],
                       {"tensor": tensor_to(i)})
 
-    def c_half(side, i, k):
-        return remote(pj.at[0, side, block(tn)], pj.at[0, side, block(tn)], c_s, c_r.at[k],
-                      {"tensor": tensor_to(i)})
-
-    for k, side in ((0, 1 - core), (1, core)):
-        for i in range(1, 8):
-            c_half(side, i, k).start()
-    for i in range(1, 8):
-        c_copy(i).start()
+    def c_wait(k):
+        with jax.named_scope("c_wait"):
+            arrive(pj.at[0, 0, 0:7 * own], c_r.at[k])
+
+    for u in range(2):
+        project_half(u)
+        done = acc[...].astype(jnp.bfloat16)
+        for c in range(2):
+            pj[u, c, block(tn)] = done[c * own:(c + 1) * own]
+        for k in (2 * u, 2 * u + 1):
+            for i in range(1, 8):
+                c_copy(u, (core + 1 + k) % 2, i, k).start()
     arrive(grad, grad_sem)
     e_near.wait_recv()
     for i in Z_ORDER:
@@ -192,7 +191,7 @@
         for s in range(0, cols, STEP):
             w = min(STEP, cols - s)
             res[n, side, :, :, :, s:s + w] = jnp.dot(
-                pj[0, side], grad[n, :, s:s + w], preferred_element_type=jnp.float32
+                pj[n // CHUNKS, side], grad[n % CHUNKS, :, s:s + w], preferred_element_type=jnp.float32
             ).reshape(2, 4, own, w)
 
     def theirs(n):
@@ -201,15 +200,6 @@
 
     def mine(n):
         half_dots(n, core)
-
-    def dots(n):
-        left = pj[1].reshape(16 * own, acc.shape[1])
-        for s in range(0, cols, STEP):
-            w = min(STEP, cols - s)
-            res[n, :, :, :, :, s:s + w] = jnp.dot(
-                left, grad[n - CHUNKS, :, s:s + w], preferred_element_type=jnp.float32
-            ).reshape(2, 2, 4, own, w)
-        t_copy(n).start()
 
     def p_y(j):
         return remote(out1.at[j, 1 - yh], in1.at[j, :, 0], p_s, p_r.at[j], at_chip(4))
@@ -358,15 +348,14 @@
 
         lax.fori_loop(0, steps, body, 0)
 
-    with jax.named_scope("c_wait0"):
-        arrive(pj.at[0, 0, 0:7 * own], c_r.at[0])
+    c_wait(0)
     loop(CHUNKS, ("theirs", theirs, 0, 0, CHUNKS))
-    with jax.named_scope("c_wait1"):
-        arrive(pj.at[0, 0, 0:7 * own], c_r.at[1])
+    c_wait(1)
     loop(CHUNKS, ("dots", mine, 0, 0, CHUNKS), ("combine", combine, 0, 0, CHUNKS))
-    with jax.named_scope("c_wait1"):
-        arrive(pj.at[1, :, 0:7 * own], c_r.at[2])
-    loop(CHUNKS + max(LAGS[:2]), ("dots", dots, 0, CHUNKS, CHUNKS), ("combine", combine, LAGS[0], CHUNKS, CHUNKS),
+    c_wait(2)
+    loop(CHUNKS, ("theirs", theirs, 0, CHUNKS, CHUNKS))
+    c_wait(3)
+    loop(CHUNKS + LAGS[1], ("dots", mine, 0, CHUNKS, CHUNKS), ("combine", combine, 0, CHUNKS, CHUNKS),
          ("one", stage_one, LAGS[1], 0, CHUNKS))
     first_copy.wait()
     second_copy.wait()
@@ -375,8 +364,8 @@
 
     with jax.named_scope("finish"):
         arrive(part.at[0:7 * rows], a_s)
-        arrive(slices.at[0:8], b_s)
-        arrive(slices.at[0:7], f_s)
+        arrive(slices.at[0], b_s)
+        arrive(slices.at[0, 0:14], f_s)
         arrive(pj.at[:, :, 0:7 * own], c_s)
         e_near.wait_send()
         arrive(basis.at[0:6 * rows], e_s)
@@ -444,8 +433,8 @@
             pltpu.VMEM((rows * 8, 128), bf),
             pltpu.VMEM(first_moment.shape, f32),
             pltpu.VMEM(second_moment.shape, f32),
-            pltpu.VMEM((16, rank // 8, width // 16), bf),
-            pltpu.VMEM((rank // 8, tokens), f32),
+            pltpu.VMEM((2, 16, rank // 16, width // 16), bf),
+            pltpu.VMEM((rank // 16, tokens), f32),
             pltpu.VMEM((2, 2, half // 2, tokens), bf),
             pltpu.VMEM((UNITS, 2, 2, 4, own, cols), f32),
             pltpu.VMEM((UNITS, 2, 4, own, cols), f32),
@@ -455,7 +444,7 @@
             pltpu.VMEM((UNITS, 4, own, cols), bf),
             pltpu.VMEM((UNITS, 14, own, cols), bf),
             dma((16,)), dma, dma((3,)), dma((8,)), dma((5,)),
-            dma((8,)), dma((8,)), dma((3,)), dma((UNITS,)),
+            dma((2, 8)), dma((2, 8)), dma((4,)), dma((UNITS,)),
             dma((UNITS,)), dma((UNITS,)), dma((UNITS,)), dma((UNITS,)),
         ],
         compiler_params=pltpu.CompilerParams(

time: 74.2 us -> 71.9 us (0.969)
  Pallas kernels: 73.4 us -> 71 us
    pallas_call x1, Pallas kernels: 69 us -> 66.6 us  [per_device(): pl.pallas_call(fused, out_shape=(pltpu.VMEM((UNITS, 2, 2, 4, own, cols),...]
where the time goes in v4:
time: 71.9 us; the launch traced here: 71.7 us
  Pallas kernels  71 us (99%)
    pallas_call x1, Pallas kernels, per_device(): pl.pallas_call(fused, out_shape=(pltpu.VMEM((UNITS, 2, 2, 4, own, cols),...  66.6 us
    pallas_call x1, Pallas kernels, per_device(): pl.pallas_call(decode, out_shape=(jax.ShapeDtypeStruct((rows * 8, ff), f3...  4.39 us

profile of v4, /device:TPU:1, one launch (start us, length us, event | category | flops | bytes accessed | tf_op | source)
XLA Modules:
  0.0 71.7 jit_solution(10474249530714606362)
XLA Ops:
  0.6 66.6 %fused.1 = (bf16[14,2,2,4,16,512]{5,4,3,2,1,0:T(8,128)(2,1)S(1)}, bf16[512,512]{1,0:T(8,128)(2,1)S(1)}, f32[32,3584]{1,0:T(8,128)S(1)}, f32[32,3584]{1,0:T(8,128)S(1)}) custom-call(bf16[1024,8192]{1,0:T(8,128)(2,1)} %act_hbm.1, bf16[1024,3584]{1,0:T(8,128)(2,1)} %grad_hbm.1, bf16[64,512]{1,0:T(8,128)(2,1)} %proj_hbm.1, f32[32,3584]{1,0:T(8,128)} %first_hbm.1, ...), custom_call_target="tpu_custom_call" | custom-call | tf_op jit(solution)/shard_map/fused/pallas_call | solution.py:419
  67.3 4.4 %decode.1 = (f32[512,3584]{1,0:T(8,128)}, f32[32,3584]{1,0:T(8,128)}, f32[32,3584]{1,0:T(8,128)}) custom-call(bf16[512,512]{1,0:T(8,128)(2,1)S(1)} %get-tuple-element.7.basis, bf16[14,2,2,4,16,512]{5,4,3,2,1,0:T(8,128)(2,1)S(1)} %get-tuple-element.8.norm, f32[32,3584]{1,0:T(8,128)S(1)} %get-tuple-element.9.nf, f32[32,3584]{1,0:T(8,128)S(1)} %get-tuple-element.10.ns), custom_call_target="tpu_custom_call" | custom-call | tf_op jit(solution)/shard_map/decode/pallas_call | solution.py:454

commit v5 on v4

--- a/solution.py
+++ b/solution.py
@@ -19,7 +19,7 @@
 UNITS = 2 * CHUNKS
 STEP = 256
 LAGS = (2, 1, 0, 7, 13)
-SLOTS = 3
+SLOTS = 4
 NT = (((1,), (1,)), ((), ()))
 
 
@@ -396,9 +396,9 @@
         out_copy(j).start()
         return 0
 
-    lax.fori_loop(0, CHUNKS, step, 0)
     nf_copy.start()
     ns_copy.start()
+    lax.fori_loop(0, CHUNKS, step, 0)
     for j in range(CHUNKS - SLOTS, CHUNKS):
         out_copy(j).wait()
     nf_copy.wait()

time: 71.9 us -> 71.6 us (level)
  no operation moved by 1% of the time
where the time goes in v5:
time: 71.6 us; the launch traced here: 71.4 us
  Pallas kernels  70.7 us (99%)
    pallas_call x1, Pallas kernels, per_device(): pl.pallas_call(fused, out_shape=(pltpu.VMEM((UNITS, 2, 2, 4, own, cols),...  66.6 us
    pallas_call x1, Pallas kernels, per_device(): pl.pallas_call(decode, out_shape=(jax.ShapeDtypeStruct((rows * 8, ff), f3...  4.11 us

profile of v5, /device:TPU:1, one launch (start us, length us, event | category | flops | bytes accessed | tf_op | source)
XLA Modules:
  0.0 71.4 jit_solution(8828823709609807937)
XLA Ops:
  0.6 66.6 %fused.1 = (bf16[14,2,2,4,16,512]{5,4,3,2,1,0:T(8,128)(2,1)S(1)}, bf16[512,512]{1,0:T(8,128)(2,1)S(1)}, f32[32,3584]{1,0:T(8,128)S(1)}, f32[32,3584]{1,0:T(8,128)S(1)}) custom-call(bf16[1024,8192]{1,0:T(8,128)(2,1)} %act_hbm.1, bf16[1024,3584]{1,0:T(8,128)(2,1)} %grad_hbm.1, bf16[64,512]{1,0:T(8,128)(2,1)} %proj_hbm.1, f32[32,3584]{1,0:T(8,128)} %first_hbm.1, ...), custom_call_target="tpu_custom_call" | custom-call | tf_op jit(solution)/shard_map/fused/pallas_call | solution.py:419
  67.3 4.1 %decode.1 = (f32[512,3584]{1,0:T(8,128)}, f32[32,3584]{1,0:T(8,128)}, f32[32,3584]{1,0:T(8,128)}) custom-call(bf16[512,512]{1,0:T(8,128)(2,1)S(1)} %get-tuple-element.7.basis, bf16[14,2,2,4,16,512]{5,4,3,2,1,0:T(8,128)(2,1)S(1)} %get-tuple-element.8.norm, f32[32,3584]{1,0:T(8,128)S(1)} %get-tuple-element.9.nf, f32[32,3584]{1,0:T(8,128)S(1)} %get-tuple-element.10.ns), custom_call_target="tpu_custom_call" | custom-call | tf_op jit(solution)/shard_map/decode/pallas_call | solution.py:454
